TPU v7x, 32 devices: a whole 2x2x4 slice. The times are simulated.
32 devices in a mesh: gz: 16 (over z, y, core), xy: 2 (over x).
Axes of the slice: x: 2, y: 2, z: 4, core: 2. Of those that a mesh axis runs over, the one named last changes fastest.
Arguments:
- fields: float32 [2, 1024, 64, 256], P(None, 'gz', 'xy'), may hold values from -64 to 64, as said below
- threshold: float32 [2], replicated, may hold values from 0.1 to 0.6
Outputs:
- detail_one: float32 [2, 512, 64, 256], P(None, 'gz', 'xy')
- detail_two: float32 [2, 256, 64, 256], P(None, 'gz', 'xy')
- detail_three: float32 [2, 128, 64, 256], P(None, 'gz', 'xy')
- detail_four: float32 [2, 64, 64, 256], P(None, 'gz', 'xy')
- detail_five: float32 [2, 32, 64, 256], P(None, 'gz', 'xy')
- coarse: float32 [2, 32, 64, 256], P(None, 'gz', 'xy')
- band_energy: float32 [2, 6], replicated
Inputs may be any that keep to these rules, and one draw needn't show every extreme that they name: Finite values; the spread of the fields varies over the grid.
All inputs are finite; a program needn't handle non-finite values.
Results may differ from a plain program's by a relative error of at most 0.00002.
Values sent between devices are 32-bit elements; how exact they have to be, the bound alone decides.
A program may use at most 64 MiB of HBM per device.

v0:
```python
import jax
import jax.numpy as jnp
from jax import lax
from jax.sharding import PartitionSpec as P

ALPHA = -1.586134342059924
BETA = -0.052980118572961
GAMMA = 0.882911075530934
DELTA = 0.443506852043971
KAPPA = 1.230174104914001
SQRT_TWO = 1.4142135623730951


def extended_2(block, sides, width):
    for axis, dim in sides:
        count = lax.axis_size(axis)
        forward = [(i, i + 1) for i in range(count - 1)]
        backward = [(target, source) for source, target in forward]
        low = lax.ppermute(
            lax.slice_in_dim(block, block.shape[dim] - width, None, axis=dim), axis, forward
        )
        high = lax.ppermute(lax.slice_in_dim(block, 0, width, axis=dim), axis, backward)
        block = jnp.concatenate([low, block, high], axis=dim)
    return block


def right_of(evens):
    return jnp.concatenate([evens[:, 1:], evens[:, -1:]], axis=1)


def left_of(odds):
    return jnp.concatenate([odds[:, :1], odds[:, :-1]], axis=1)


def one_level(values):
    half = values.shape[1] // 2
    paired = values.reshape(values.shape[0], half, 2, values.shape[2], values.shape[3])
    evens = paired[:, :, 0]
    odds = paired[:, :, 1]
    odds = odds + ALPHA * (evens + right_of(evens))
    evens = evens + BETA * (left_of(odds) + odds)
    odds = odds + GAMMA * (evens + right_of(evens))
    evens = evens + DELTA * (left_of(odds) + odds)
    return (evens * (SQRT_TWO / KAPPA), odds * (KAPPA / SQRT_TWO))


def shrink(band, limit):
    return band - jnp.clip(band, -limit, limit)


def rim_level(values):
    length = values.shape[1]
    extended = extended_2(values, (("gz", 1),), 4)
    position = lax.axis_index("gz")
    count = lax.axis_size("gz")
    lower = jnp.where(position == 0, extended[:, 8:4:-1], extended[:, 0:4])
    upper = jnp.where(
        position == count - 1,
        extended[:, length + 2 : length - 2 : -1],
        extended[:, length + 4 : length + 8],
    )
    extended = jnp.concatenate([lower, extended[:, 4 : length + 4], upper], axis=1)
    approx, detail = one_level(extended)
    pairs = length // 2
    return (approx[:, 2 : 2 + pairs], detail[:, 2 : 2 + pairs])


def local(fields, threshold):
    limit = threshold.reshape(2, 1, 1, 1)
    bands = []
    approx = fields
    for level in range(5):
        approx, detail = rim_level(approx)
        bands.append(shrink(detail, limit))
    bands.append(shrink(approx, limit))
    partial_sums = jnp.stack([jnp.sum(band * band, axis=(1, 2, 3)) for band in bands], axis=1)
    totals = lax.psum(partial_sums, ("gz", "xy"))
    devices_all = lax.axis_size("gz") * lax.axis_size("xy")
    cells = jnp.array(
        [band.shape[1] * band.shape[2] * band.shape[3] * devices_all for band in bands], jnp.float32
    )
    energy = totals / cells[None, :]
    return (bands[0], bands[1], bands[2], bands[3], bands[4], bands[5], energy)


def solution(mesh):
    placed = (P(None, "gz", "xy", None), P())
    return jax.shard_map(
        local,
        mesh=mesh,
        in_specs=placed,
        out_specs=(
            P(None, "gz", "xy", None),
            P(None, "gz", "xy", None),
            P(None, "gz", "xy", None),
            P(None, "gz", "xy", None),
            P(None, "gz", "xy", None),
            P(None, "gz", "xy", None),
            P(),
        ),
        check_vma=False,
    )
```

profile of v0, /device:TPU:0, one launch (start us, length us, event | category | flops | bytes accessed | tf_op | source)
XLA Modules:
  0.0 117.6 jit_solution(6481950627521044520)
XLA Ops:
  0.6 1.3 %fusion.45 = (f32[2,4,32,256]{3,2,1,0:T(8,128)S(1)}, f32[2,4,32,256]{3,2,1,0:T(8,128)S(1)}, f32[2,4,32,256]{3,2,1,0:T(8,128)S(1)}, f32[2,4,32,256]{3,2,1,0:T(8,128)S(1)}) fusion(f32[2,64,32,256]{3,2,1,0:T(8,128)} %param.3), kind=kLoop, calls=%fused_computation.110 | loop fusion | bytes 2097152 | tf_op jit(solution)/shard_map/slice | solution.py:56
  1.9 2.4 %collective-permute-start = (f32[2,4,32,256]{3,2,1,0:T(8,128)S(1)}, f32[2,4,32,256]{3,2,1,0:T(8,128)S(1)}, u32[]{:S(2)}, u32[]{:S(2)}) collective-permute-start(f32[2,4,32,256]{3,2,1,0:T(8,128)S(1)} %get-tuple-element.42), channel_id=1, source_target_pairs={{0,2},{2,4},{4,6},{6,8},{8,10},{10,12},{12,14},{14,16},{16,18},{18... | collective-permute-start | bytes 786440 | tf_op jit(solution)/shard_map/ppermute | solution.py:19
  4.3 1.3 %collective-permute-start.1 = (f32[2,4,32,256]{3,2,1,0:T(8,128)S(1)}, f32[2,4,32,256]{3,2,1,0:T(8,128)S(1)}, u32[]{:S(2)}, u32[]{:S(2)}) collective-permute-start(f32[2,4,32,256]{3,2,1,0:T(8,128)S(1)} %get-tuple-element.43), channel_id=1, source_target_pairs={{2,0},{4,2},{6,4},{8,6},{10,8},{12,10},{14,12},{16,14},{18,16},{20... | collective-permute-start | bytes 786440 | tf_op jit(solution)/shard_map/ppermute | solution.py:22
  5.7 4.2 %collective-permute-done.1 = f32[2,4,32,256]{3,2,1,0:T(8,128)S(1)} collective-permute-done((f32[2,4,32,256]{3,2,1,0:T(8,128)S(1)}, f32[2,4,32,256]{3,2,1,0:T(8,128)S(1)}, u32[]{:S(2)}, u32[]{:S(2)}) %collective-permute-start.1) | collective-permute-done | bytes 262176 | tf_op jit(solution)/shard_map/ppermute | solution.py:22
  9.9 2.6 %pad_maximum_fusion = f32[2,72,32,256]{3,2,1,0:T(8,128)S(1)} fusion(f32[2,4,32,256]{3,2,1,0:T(8,128)S(1)} %reverse_select_fusion.8, f32[2,64,32,256]{3,2,1,0:T(8,128)} %param.3, f32[2,4,32,256]{3,2,1,0:T(8,128)S(1)} %reverse_select_fusion.9), kind=kLoop, calls=%fused_computation | loop fusion | flops 2359296 | bytes 9437184 | tf_op jit(solution)/shard_map/concatenate | solution.py:62
  13.0 0.8 fusion
  14.1 0.8 fusion.3
  15.2 1.0 fusion.5
  16.5 1.1 fusion.8
  17.7 6.7 %collective-permute-start.2 = (f32[2,4,32,256]{3,2,1,0:T(8,128)S(1)}, f32[2,4,32,256]{3,2,1,0:T(8,128)S(1)}, u32[]{:S(2)}, u32[]{:S(2)}) collective-permute-start(f32[2,4,32,256]{3,2,1,0:T(8,128)S(1)} %get-tuple-element.47), channel_id=1, source_target_pairs={{0,2},{2,4},{4,6},{6,8},{8,10},{10,12},{12,14},{14,16},{16,18},{18... | collective-permute-start | bytes 786440 | tf_op jit(solution)/shard_map/ppermute | solution.py:19
  24.3 1.3 %collective-permute-start.3 = (f32[2,4,32,256]{3,2,1,0:T(8,128)S(1)}, f32[2,4,32,256]{3,2,1,0:T(8,128)S(1)}, u32[]{:S(2)}, u32[]{:S(2)}) collective-permute-start(f32[2,4,32,256]{3,2,1,0:T(8,128)S(1)} %get-tuple-element.45), channel_id=1, source_target_pairs={{2,0},{4,2},{6,4},{8,6},{10,8},{12,10},{14,12},{16,14},{18,16},{20... | collective-permute-start | bytes 786440 | tf_op jit(solution)/shard_map/ppermute | solution.py:22
  25.8 1.9 %collective-permute-done.3 = f32[2,4,32,256]{3,2,1,0:T(8,128)S(1)} collective-permute-done((f32[2,4,32,256]{3,2,1,0:T(8,128)S(1)}, f32[2,4,32,256]{3,2,1,0:T(8,128)S(1)}, u32[]{:S(2)}, u32[]{:S(2)}) %collective-permute-start.3) | collective-permute-done | bytes 262176 | tf_op jit(solution)/shard_map/ppermute | solution.py:22
  28.4 0.4 fusion.9
  28.9 0.4 fusion.12
  30.1 0.5 fusion.17
  30.6 7.0 %collective-permute-start.4 = (f32[2,4,32,256]{3,2,1,0:T(8,128)S(1)}, f32[2,4,32,256]{3,2,1,0:T(8,128)S(1)}, u32[]{:S(2)}, u32[]{:S(2)}) collective-permute-start(f32[2,4,32,256]{3,2,1,0:T(8,128)S(1)} %get-tuple-element.51), channel_id=1, source_target_pairs={{0,2},{2,4},{4,6},{6,8},{8,10},{10,12},{12,14},{14,16},{16,18},{18... | collective-permute-start | bytes 786440 | tf_op jit(solution)/shard_map/ppermute | solution.py:19
  37.6 1.3 %collective-permute-start.5 = (f32[2,4,32,256]{3,2,1,0:T(8,128)S(1)}, f32[2,4,32,256]{3,2,1,0:T(8,128)S(1)}, u32[]{:S(2)}, u32[]{:S(2)}) collective-permute-start(f32[2,4,32,256]{3,2,1,0:T(8,128)S(1)} %get-tuple-element.49), channel_id=1, source_target_pairs={{2,0},{4,2},{6,4},{8,6},{10,8},{12,10},{14,12},{16,14},{18,16},{20... | collective-permute-start | bytes 786440 | tf_op jit(solution)/shard_map/ppermute | solution.py:22
  39.1 2.0 %collective-permute-done.5 = f32[2,4,32,256]{3,2,1,0:T(8,128)S(1)} collective-permute-done((f32[2,4,32,256]{3,2,1,0:T(8,128)S(1)}, f32[2,4,32,256]{3,2,1,0:T(8,128)S(1)}, u32[]{:S(2)}, u32[]{:S(2)}) %collective-permute-start.5) | collective-permute-done | bytes 262176 | tf_op jit(solution)/shard_map/ppermute | solution.py:22
  42.4 0.9 fusion.48
  43.4 7.8 %collective-permute-start.6 = (f32[2,4,32,256]{3,2,1,0:T(8,128)}, f32[2,4,32,256]{3,2,1,0:T(8,128)}, u32[]{:S(2)}, u32[]{:S(2)}) collective-permute-start(f32[2,4,32,256]{3,2,1,0:T(8,128)} %get-tuple-element.55), channel_id=1, source_target_pairs={{0,2},{2,4},{4,6},{6,8},{8,10},{10,12},{12,14},{14,16},{16,18},{18... | collective-permute-start | bytes 786440 | tf_op jit(solution)/shard_map/ppermute | solution.py:19
  51.1 1.3 %collective-permute-start.7 = (f32[2,4,32,256]{3,2,1,0:T(8,128)}, f32[2,4,32,256]{3,2,1,0:T(8,128)}, u32[]{:S(2)}, u32[]{:S(2)}) collective-permute-start(f32[2,4,32,256]{3,2,1,0:T(8,128)} %get-tuple-element.53), channel_id=1, source_target_pairs={{2,0},{4,2},{6,4},{8,6},{10,8},{12,10},{14,12},{16,14},{18,16},{20... | collective-permute-start | bytes 786440 | tf_op jit(solution)/shard_map/ppermute | solution.py:22
  52.4 1.8 %multiply_reduce_fusion = (f32[2]{0:T(128)S(1)}, f32[2,32,32,256]{3,2,1,0:T(8,128)}) fusion(f32[2]{0:T(128)S(1)} %neg.3, f32[2]{0:T(128)S(1)} %copy-done, f32[2,36,32,256]{3,2,1,0:T(8,128)S(1)} %fusion.5), kind=kLoop, calls=%fused_computation.18 | loop fusion | flops 3145726 | bytes 4194328 | tf_op jit(solution)/shard_map/reduce_sum | solution.py:76
  54.4 0.5 collective-permute-done.7
  54.9 1.0 reverse_select_fusion.2
  56.6 0.9 multiply_reduce_fusion.3
  57.5 1.3 %collective-permute-start.8 = (f32[2,4,32,256]{3,2,1,0:T(8,128)S(1)}, f32[2,4,32,256]{3,2,1,0:T(8,128)S(1)}, u32[]{:S(2)}, u32[]{:S(2)}) collective-permute-start(f32[2,4,32,256]{3,2,1,0:T(8,128)S(1)} %get-tuple-element.56), channel_id=1, source_target_pairs={{2,0},{4,2},{6,4},{8,6},{10,8},{12,10},{14,12},{16,14},{18,16},{20... | collective-permute-start | bytes 786440 | tf_op jit(solution)/shard_map/ppermute | solution.py:22
  58.8 1.3 %multiply_reduce_fusion.1 = (f32[2]{0:T(128)S(1)}, f32[2,16,32,256]{3,2,1,0:T(8,128)}) fusion(f32[2]{0:T(128)S(1)} %neg.3, f32[2]{0:T(128)S(1)} %copy-done, f32[2,20,32,256]{3,2,1,0:T(8,128)S(1)} %fusion.14), kind=kLoop, calls=%fused_computation.38 | loop fusion | flops 1572862 | bytes 2097176 | tf_op jit(solution)/shard_map/reduce_sum | solution.py:76
  60.1 7.0 %collective-permute-start.9 = (f32[2,4,32,256]{3,2,1,0:T(8,128)S(1)}, f32[2,4,32,256]{3,2,1,0:T(8,128)S(1)}, u32[]{:S(2)}, u32[]{:S(2)}) collective-permute-start(f32[2,4,32,256]{3,2,1,0:T(8,128)S(1)} %get-tuple-element.56), channel_id=1, source_target_pairs={{0,2},{2,4},{4,6},{6,8},{8,10},{10,12},{12,14},{14,16},{16,18},{18... | collective-permute-start | bytes 786440 | tf_op jit(solution)/shard_map/ppermute | solution.py:19
  67.1 1.0 multiply_reduce_fusion.2
  69.0 0.8 multiply_reduce_fusion.4
  70.1 46.9 %psum.7 = f32[2,6]{1,0:T(2,128)S(1)} all-reduce(f32[2,6]{1,0:T(2,128)S(1)} %stack.27), channel_id=1, replica_groups=mesh['gz'=16,'xy'=2] {'gz','xy'}, use_global_device_ids=true, to_apply=%region_6.7 | all-reduce | flops 12 | bytes 96 | tf_op jit(solution)/shard_map/psum | solution.py:77
  117.0 0.6 broadcast_multiply_fusion
  (93 shorter events, 6.5 us)
Async XLA Ops:
  1.9 3.7 %collective-permute-start = (f32[2,4,32,256]{3,2,1,0:T(8,128)S(1)}, f32[2,4,32,256]{3,2,1,0:T(8,128)S(1)}, u32[]{:S(2)}, u32[]{:S(2)}) collective-permute-start(f32[2,4,32,256]{3,2,1,0:T(8,128)S(1)} %get-tuple-element.42), channel_id=1, source_target_pairs={{0,2},{2,4},{4,6},{6,8},{8,10},{10,12},{12,14},{14,16},{16,18},{18... | collective-permute-start | bytes 786440 | tf_op jit(solution)/shard_map/ppermute | solution.py:19
  4.3 5.5 %collective-permute-start.1 = (f32[2,4,32,256]{3,2,1,0:T(8,128)S(1)}, f32[2,4,32,256]{3,2,1,0:T(8,128)S(1)}, u32[]{:S(2)}, u32[]{:S(2)}) collective-permute-start(f32[2,4,32,256]{3,2,1,0:T(8,128)S(1)} %get-tuple-element.43), channel_id=1, source_target_pairs={{2,0},{4,2},{6,4},{8,6},{10,8},{12,10},{14,12},{16,14},{18,16},{20... | collective-permute-start | bytes 786440 | tf_op jit(solution)/shard_map/ppermute | solution.py:22
  17.7 8.1 %collective-permute-start.2 = (f32[2,4,32,256]{3,2,1,0:T(8,128)S(1)}, f32[2,4,32,256]{3,2,1,0:T(8,128)S(1)}, u32[]{:S(2)}, u32[]{:S(2)}) collective-permute-start(f32[2,4,32,256]{3,2,1,0:T(8,128)S(1)} %get-tuple-element.47), channel_id=1, source_target_pairs={{0,2},{2,4},{4,6},{6,8},{8,10},{10,12},{12,14},{14,16},{16,18},{18... | collective-permute-start | bytes 786440 | tf_op jit(solution)/shard_map/ppermute | solution.py:19
  24.3 3.4 %collective-permute-start.3 = (f32[2,4,32,256]{3,2,1,0:T(8,128)S(1)}, f32[2,4,32,256]{3,2,1,0:T(8,128)S(1)}, u32[]{:S(2)}, u32[]{:S(2)}) collective-permute-start(f32[2,4,32,256]{3,2,1,0:T(8,128)S(1)} %get-tuple-element.45), channel_id=1, source_target_pairs={{2,0},{4,2},{6,4},{8,6},{10,8},{12,10},{14,12},{16,14},{18,16},{20... | collective-permute-start | bytes 786440 | tf_op jit(solution)/shard_map/ppermute | solution.py:22
  30.0 8.9 %copy-start = (f32[2]{0:T(128)S(1)}, f32[2]{0:T(128)}, u32[]{:S(2)}) copy-start(f32[2]{0:T(128)} %param.4) | copy-start | bytes 28
  30.6 8.4 %collective-permute-start.4 = (f32[2,4,32,256]{3,2,1,0:T(8,128)S(1)}, f32[2,4,32,256]{3,2,1,0:T(8,128)S(1)}, u32[]{:S(2)}, u32[]{:S(2)}) collective-permute-start(f32[2,4,32,256]{3,2,1,0:T(8,128)S(1)} %get-tuple-element.51), channel_id=1, source_target_pairs={{0,2},{2,4},{4,6},{6,8},{8,10},{10,12},{12,14},{14,16},{16,18},{18... | collective-permute-start | bytes 786440 | tf_op jit(solution)/shard_map/ppermute | solution.py:19
  37.6 3.4 %collective-permute-start.5 = (f32[2,4,32,256]{3,2,1,0:T(8,128)S(1)}, f32[2,4,32,256]{3,2,1,0:T(8,128)S(1)}, u32[]{:S(2)}, u32[]{:S(2)}) collective-permute-start(f32[2,4,32,256]{3,2,1,0:T(8,128)S(1)} %get-tuple-element.49), channel_id=1, source_target_pairs={{2,0},{4,2},{6,4},{8,6},{10,8},{12,10},{14,12},{16,14},{18,16},{20... | collective-permute-start | bytes 786440 | tf_op jit(solution)/shard_map/ppermute | solution.py:22
  43.4 11.0 %collective-permute-start.6 = (f32[2,4,32,256]{3,2,1,0:T(8,128)}, f32[2,4,32,256]{3,2,1,0:T(8,128)}, u32[]{:S(2)}, u32[]{:S(2)}) collective-permute-start(f32[2,4,32,256]{3,2,1,0:T(8,128)} %get-tuple-element.55), channel_id=1, source_target_pairs={{0,2},{2,4},{4,6},{6,8},{8,10},{10,12},{12,14},{14,16},{16,18},{18... | collective-permute-start | bytes 786440 | tf_op jit(solution)/shard_map/ppermute | solution.py:19
  51.1 3.8 %collective-permute-start.7 = (f32[2,4,32,256]{3,2,1,0:T(8,128)}, f32[2,4,32,256]{3,2,1,0:T(8,128)}, u32[]{:S(2)}, u32[]{:S(2)}) collective-permute-start(f32[2,4,32,256]{3,2,1,0:T(8,128)} %get-tuple-element.53), channel_id=1, source_target_pairs={{2,0},{4,2},{6,4},{8,6},{10,8},{12,10},{14,12},{16,14},{18,16},{20... | collective-permute-start | bytes 786440 | tf_op jit(solution)/shard_map/ppermute | solution.py:22
  57.5 10.8 %collective-permute-start.8 = (f32[2,4,32,256]{3,2,1,0:T(8,128)S(1)}, f32[2,4,32,256]{3,2,1,0:T(8,128)S(1)}, u32[]{:S(2)}, u32[]{:S(2)}) collective-permute-start(f32[2,4,32,256]{3,2,1,0:T(8,128)S(1)} %get-tuple-element.56), channel_id=1, source_target_pairs={{2,0},{4,2},{6,4},{8,6},{10,8},{12,10},{14,12},{16,14},{18,16},{20... | collective-permute-start | bytes 786440 | tf_op jit(solution)/shard_map/ppermute | solution.py:22
  60.1 8.2 %collective-permute-start.9 = (f32[2,4,32,256]{3,2,1,0:T(8,128)S(1)}, f32[2,4,32,256]{3,2,1,0:T(8,128)S(1)}, u32[]{:S(2)}, u32[]{:S(2)}) collective-permute-start(f32[2,4,32,256]{3,2,1,0:T(8,128)S(1)} %get-tuple-element.56), channel_id=1, source_target_pairs={{0,2},{2,4},{4,6},{6,8},{8,10},{10,12},{12,14},{14,16},{16,18},{18... | collective-permute-start | bytes 786440 | tf_op jit(solution)/shard_map/ppermute | solution.py:19
  68.8 48.2 %copy-start.1 = (f32[6]{0:T(128)S(1)}, f32[6]{0:T(128)}, u32[]{:S(2)}) copy-start(f32[6]{0:T(128)} %constant.3) | copy-start | bytes 76
where the time goes:
time: 118 us
  blocking collectives  46.9 us (40%)
  starting transfers between devices  37.3 us (32%)
  other arithmetic  17.6 us (15%)
  waiting for transfers between devices  8.55 us (7%)
  local copies, waits for them, and re-layouts  5.83 us (5%)
  between operations  1.39 us (1%)
    psum x1, blocking collectives, local(): totals = lax.psum(partial_sums, ('gz', 'xy'))  46.9 us
    ppermute x5, starting transfers between devices, extended_2(): lax.ppermute(lax.slice_in_dim(block, block.shape[dim] - width, None, axis...  30.8 us
    ppermute x5, waiting for transfers between devices, extended_2(): lax.ppermute(lax.slice_in_dim(block, 0, width, axis=dim), axis, backward)  8.54 us
    ppermute x5, starting transfers between devices, extended_2(): lax.ppermute(lax.slice_in_dim(block, 0, width, axis=dim), axis, backward)  6.44 us
    reduce_sum x5, other arithmetic, local(): jnp.sum(band * band, axis=(1, 2, 3))  5.73 us
    concatenate x5, other arithmetic, rim_level(): jnp.concatenate([lower, extended[:, 4:length + 4], upper], axis=1)  3.26 us
    slice x4, local copies, waits for them, and re-layouts, rim_level(): lower = jnp.where(position == 0, extended[:, 8:4:-1], extended[:, 0:4])  2.39 us
  transfers between devices with their start and end apart: 10, of which 4 were waited for; matrix products, arithmetic and copies ran while one was open for 4% of the time, Pallas kernels for 0%

commit v1 on v0

v1 whole, which is shorter than its diff:
```python
import functools

import jax
import jax.numpy as jnp
from jax import lax
from jax.experimental import pallas as pl
from jax.experimental.pallas import tpu as pltpu
from jax.sharding import PartitionSpec as P

ALPHA = -1.586134342059924
BETA = -0.052980118572961
GAMMA = 0.882911075530934
DELTA = 0.443506852043971
KAPPA = 1.230174104914001
SQRT_TWO = 1.4142135623730951
LEVELS = 5
MESH = pl.DeviceIdType.MESH
UP, DOWN = 0, 1
SUB = 8
ROWS = 8


def kernel(
    gz_count,
    xy_count,
    threshold_ref,
    fields_ref,
    *refs,
):
    outs = refs[: LEVELS + 1]
    energy_ref = refs[LEVELS + 1]
    inputs = refs[LEVELS + 2 : 2 * LEVELS + 2]
    send_buf, recv_buf, acc, e_send_buf, e_recv_buf = refs[2 * LEVELS + 2 : 2 * LEVELS + 7]
    in_sem, edge_sem, send_sem, recv_sem, e_send_sem, e_recv_sem = refs[2 * LEVELS + 7 :]
    field_count, layers, width, _ = fields_ref.shape
    per_field = width // ROWS
    chunks = field_count * per_field
    devices = gz_count * xy_count

    gz = lax.axis_index("gz")
    xy = lax.axis_index("xy")
    me = gz * xy_count + xy
    first = gz == 0
    last = gz == gz_count - 1
    not_first = gz > 0
    not_last = gz < gz_count - 1

    def peer(step):
        target = lax.rem(me + step, devices)
        return (target // xy_count, lax.rem(target, xy_count))

    barrier = pltpu.get_barrier_semaphore()

    @pl.loop(1, devices)
    def _(step):
        pl.semaphore_signal(barrier, inc=1, device_id=peer(step), device_id_type=MESH)

    def place(c):
        return c // per_field, pl.multiple_of(lax.rem(c, per_field) * ROWS, ROWS)

    def edge_copy(side):
        part = pl.ds(0 if side == 0 else layers - 4, 4)
        return pltpu.make_async_copy(
            fields_ref.at[:, part], inputs[0].at[:, part], edge_sem.at[side]
        )

    def body_copy(c):
        f, row = place(c)
        where = (f, pl.ds(4, layers - 8), pl.ds(row, ROWS))
        return pltpu.make_async_copy(
            fields_ref.at[where], inputs[0].at[where], in_sem.at[c]
        )

    edge_copy(0).start()
    edge_copy(1).start()

    @pl.loop(0, chunks)
    def _(c):
        body_copy(c).start()

    acc[...] = jnp.zeros_like(acc)

    def send_states(level, c):
        source = inputs[level]
        count = source.shape[1]
        f, row = place(c)
        for t in range(ROWS // SUB):
            at = pl.ds(pl.multiple_of(row + t * SUB, SUB), SUB)
            to = pl.ds(t * SUB, SUB)
            s_head, d_head, s_after = (source[f, j, at] for j in range(3))
            s_prev, d_prev, s_tail, d_tail = (source[f, count - 4 + j, at] for j in range(4))
            send_buf[level, UP, c, 0, to] = d_tail + ALPHA * s_tail
            send_buf[level, UP, c, 1, to] = s_tail + BETA * (d_prev + ALPHA * (s_prev + s_tail))
            send_buf[level, DOWN, c, 0, to] = s_head
            send_buf[level, DOWN, c, 1, to] = s_head + BETA * (d_head + ALPHA * (s_head + s_after))

    def state_copy(level, c, way):
        return pltpu.make_async_remote_copy(
            src_ref=send_buf.at[level, way, c],
            dst_ref=recv_buf.at[level, way, c],
            send_sem=send_sem.at[level, way, c],
            recv_sem=recv_sem.at[level, way, c],
            device_id={"gz": gz + 1 if way == UP else gz - 1},
            device_id_type=MESH,
        )

    def start_states(level, c):
        @pl.when(not_last)
        def _():
            state_copy(level, c, UP).start()

        @pl.when(not_first)
        def _():
            state_copy(level, c, DOWN).start()

    def wait_states(level, c):
        @pl.when(not_first)
        def _():
            state_copy(level, c, UP).wait_recv()

        @pl.when(not_last)
        def _():
            state_copy(level, c, DOWN).wait_recv()

    def full_level(level, c):
        source = inputs[level]
        half = source.shape[1] // 2
        final = level == LEVELS - 1
        f, row = place(c)
        limit = threshold_ref[f]

        def shrink(band):
            return band - jnp.minimum(jnp.maximum(band, -limit), limit)

        for t in range(ROWS // SUB):
            at = pl.ds(pl.multiple_of(row + t * SUB, SUB), SUB)
            to = pl.ds(t * SUB, SUB)
            low_x = recv_buf[level, UP, c, 0, to]
            low_y = recv_buf[level, UP, c, 1, to]
            high_p = recv_buf[level, DOWN, c, 0, to]
            high_q = recv_buf[level, DOWN, c, 1, to]
            detail_sum = None
            coarse_sum = None
            s = source[f, 0, at]
            d1_before = s1_before = d2_before = None
            for i in range(half + 1):
                if i < half:
                    if i + 1 < half:
                        s_next = source[f, 2 * i + 2, at]
                    else:
                        s_next = jnp.where(last, s, high_p)
                    d1 = source[f, 2 * i + 1, at] + ALPHA * (s + s_next)
                    if i == 0:
                        d1_before = jnp.where(first, d1, low_x + ALPHA * s)
                    s1 = s + BETA * (d1_before + d1)
                else:
                    s1 = jnp.where(last, s1_before, high_q + BETA * d1_before)
                if i == 0:
                    outer = low_y + BETA * d1_before
                    d2_before = d1_before + GAMMA * (outer + s1)
                else:
                    d2 = d1_before + GAMMA * (s1_before + s1)
                    if i == 1:
                        d2_before = jnp.where(first, d2, d2_before)
                    s2 = s1_before + DELTA * (d2_before + d2)
                    band = shrink(d2 * (KAPPA / SQRT_TWO))
                    outs[level][f, i - 1, at] = band
                    square = band * band
                    detail_sum = square if detail_sum is None else detail_sum + square
                    approx = s2 * (SQRT_TWO / KAPPA)
                    if final:
                        band = shrink(approx)
                        outs[LEVELS][f, i - 1, at] = band
                        square = band * band
                        coarse_sum = square if coarse_sum is None else coarse_sum + square
                    else:
                        inputs[level + 1][f, i - 1, at] = approx
                    d2_before = d2
                if i < half:
                    d1_before, s1_before, s = d1, s1, s_next
            acc[f, level] += detail_sum
            if final:
                acc[f, LEVELS] += coarse_sum

    edge_copy(0).wait()
    edge_copy(1).wait()

    @pl.loop(0, chunks)
    def _(c):
        send_states(0, c)

    pl.semaphore_wait(barrier, devices - 1)

    @pl.loop(0, chunks)
    def _(c):
        start_states(0, c)

    for level in range(LEVELS):

        @pl.loop(0, chunks)
        def _(c):
            if level == 0:
                body_copy(c).wait()
            wait_states(level, c)
            full_level(level, c)
            if level + 1 < LEVELS:
                send_states(level + 1, c)
                start_states(level + 1, c)

    lane = lax.broadcasted_iota(jnp.int32, (1, 128), 1)
    for f in range(field_count):
        row = jnp.zeros((1, 128), jnp.float32)
        for b in range(LEVELS + 1):
            total = jnp.sum(jnp.sum(acc[f, b], axis=0, keepdims=True), axis=1, keepdims=True)
            row = jnp.where(lane == b, total, row)
        e_send_buf[pl.ds(f, 1), :] = row

    def energy_copy(step):
        return pltpu.make_async_remote_copy(
            src_ref=e_send_buf,
            dst_ref=e_recv_buf.at[me],
            send_sem=e_send_sem,
            recv_sem=e_recv_sem,
            device_id=peer(step),
            device_id_type=MESH,
        )

    @pl.loop(1, devices)
    def _(step):
        energy_copy(step).start()

    e_recv_buf[me] = e_send_buf[...]

    others = e_recv_buf.at[pl.ds(0, devices - 1)]
    pltpu.make_async_copy(others, others, e_recv_sem).wait()

    totals = jnp.sum(e_recv_buf[...], axis=0)
    cells = jnp.ones((1, 128), jnp.float32)
    for b in range(LEVELS + 1):
        shape = outs[b].shape
        cells = jnp.where(lane == b, float(shape[1] * shape[2] * shape[3] * devices), cells)
    energy_ref[...] = (totals / cells)[:, : LEVELS + 1]

    pltpu.make_async_copy(others, others, e_send_sem).wait()

    @pl.loop(0, chunks)
    def _(c):
        for level in range(LEVELS):

            @pl.when(not_last)
            def _():
                state_copy(level, c, UP).wait_send()

            @pl.when(not_first)
            def _():
                state_copy(level, c, DOWN).wait_send()


def solution(mesh):
    gz_count, xy_count = mesh.shape["gz"], mesh.shape["xy"]
    devices = gz_count * xy_count

    def local(fields, threshold):
        field_count, layers, width, depth = fields.shape
        chunks = field_count * (width // ROWS)
        f32 = jnp.float32
        halves = [layers >> (level + 1) for level in range(LEVELS)]
        band_layers = halves + halves[-1:]
        vmem = pl.BlockSpec(memory_space=pltpu.VMEM)
        return pl.pallas_call(
            functools.partial(kernel, gz_count, xy_count),
            out_shape=tuple(
                jax.ShapeDtypeStruct((field_count, n, width, depth), f32) for n in band_layers
            )
            + (jax.ShapeDtypeStruct((field_count, LEVELS + 1), f32),),
            in_specs=[
                pl.BlockSpec(memory_space=pltpu.SMEM),
                pl.BlockSpec(memory_space=pl.ANY),
            ],
            out_specs=(vmem,) * (LEVELS + 2),
            scratch_shapes=[
                pltpu.VMEM((field_count, n, width, depth), f32) for n in [layers] + halves[:-1]
            ]
            + [
                pltpu.VMEM((LEVELS, 2, chunks, 2, ROWS, depth), f32),
                pltpu.VMEM((LEVELS, 2, chunks, 2, ROWS, depth), f32),
                pltpu.VMEM((field_count, LEVELS + 1, SUB, depth), f32),
                pltpu.VMEM((field_count, 128), f32),
                pltpu.VMEM((devices, field_count, 128), f32),
                pltpu.SemaphoreType.DMA((chunks,)),
                pltpu.SemaphoreType.DMA((2,)),
                pltpu.SemaphoreType.DMA((LEVELS, 2, chunks)),
                pltpu.SemaphoreType.DMA((LEVELS, 2, chunks)),
                pltpu.SemaphoreType.DMA,
                pltpu.SemaphoreType.DMA,
            ],
            compiler_params=pltpu.CompilerParams(
                collective_id=0,
                has_side_effects=True,
                vmem_limit_bytes=32 * 1024 * 1024,
            ),
        )(threshold, fields)

    banded = P(None, "gz", "xy", None)
    return jax.shard_map(
        local,
        mesh=mesh,
        in_specs=(banded, P()),
        out_specs=(banded,) * (LEVELS + 1) + (P(),),
        check_vma=False,
    )
```

time: 118 us -> 38.9 us (0.33)
  blocking collectives: 46.9 us -> 0 us
  starting transfers between devices: 37.3 us -> 0 us
  Pallas kernels: 0 us -> 29.6 us
  other arithmetic: 17.6 us -> 0 us
  waiting for transfers between devices: 8.55 us -> 0 us
  local copies, waits for them, and re-layouts: 5.83 us -> 8.49 us
    psum x1 -> x0, blocking collectives: 46.9 us -> none  [local(): totals = lax.psum(partial_sums, ('gz', 'xy'))]
    ppermute x10 -> x0, starting transfers between devices: 37.3 us -> none  [the longest x5 30.8 us: extended_2(): lax.ppermute(lax.slice_in_dim(block, block.shape[dim] - width, None, axis...]
    pallas_call x0 -> x1, Pallas kernels: none -> 29.6 us  [local(): pl.pallas_call(functools.partial(kernel, gz_count, xy_count), out_shape=t...]
    ppermute x10 -> x0, waiting for transfers between devices: 8.55 us -> none  [the longest x5 8.54 us: extended_2(): lax.ppermute(lax.slice_in_dim(block, 0, width, axis=dim), axis, backward)]
    unnamed x4 -> x11, local copies, waits for them, and re-layouts: 0.01 us -> 8.49 us
    reduce_sum x5 -> x0, other arithmetic: 5.73 us -> none  [local(): jnp.sum(band * band, axis=(1, 2, 3))]
    add x15 -> x0, other arithmetic: 4.96 us -> none  [the longest x5 1.82 us: one_level(): odds = odds + GAMMA * (evens + right_of(evens))]
    slice x47 -> x0, local copies, waits for them, and re-layouts: 4.61 us -> none  [the longest x4 2.39 us: rim_level(): lower = jnp.where(position == 0, extended[:, 8:4:-1], extended[:, 0:4])]
  transfers between devices with their start and end apart: 10 -> 0, of which waited for: 4 -> 0; matrix products, arithmetic and copies ran while one was open for 4% -> 0% of each run, Pallas kernels for 0% -> 0%
where the time goes in v1:
time: 38.9 us; the launch traced here: 38.7 us
  Pallas kernels  29.6 us (76%)
  local copies, waits for them, and re-layouts  8.49 us (22%)
  between operations  0.65 us (2%)
    pallas_call x1, Pallas kernels, local(): pl.pallas_call(functools.partial(kernel, gz_count, xy_count), out_shape=t...  29.6 us
    unnamed x11, local copies, waits for them, and re-layouts  8.49 us

profile of v1, /device:TPU:0, one launch (start us, length us, event | category | flops | bytes accessed | tf_op | source)
XLA Modules:
  0.0 38.7 jit_solution(1203429648398267591)
XLA Ops:
  0.6 0.0 copy-start
  0.6 2.2 %copy-done = f32[2,64,32,256]{3,2,1,0:T(8,128)S(1)} copy-done((f32[2,64,32,256]{3,2,1,0:T(8,128)S(1)}, f32[2,64,32,256]{3,2,1,0:T(8,128)}, u32[]{:S(2)}) %copy-start) | copy-done | bytes 4194328
  2.8 0.0 copy-start.1
  2.8 0.7 %copy-done.1 = f32[2]{0:T(128)S(1)} copy-done((f32[2]{0:T(128)S(1)}, f32[2]{0:T(128)}, u32[]{:S(2)}) %copy-start.1) | copy-done | bytes 32
  3.5 29.6 %shard_map.81 = (f32[2,32,32,256]{3,2,1,0:T(8,128)S(1)}, f32[2,16,32,256]{3,2,1,0:T(8,128)S(1)}, f32[2,8,32,256]{3,2,1,0:T(8,128)S(1)}, f32[2,4,32,256]{3,2,1,0:...) custom-call(f32[2]{0:T(128)S(1)} %copy-done.1, ...), custom_call_target="tpu_custom_call" | custom-call | tf_op jit(solution)/shard_map/pallas_call | solution.py:270
  33.1 1.3 %copy.16 = f32[2,32,32,256]{3,2,1,0:T(8,128)} copy(f32[2,32,32,256]{3,2,1,0:T(8,128)S(1)} %get-tuple-element.14) | data formatting | bytes 4194304
  34.4 1.0 %copy.17 = f32[2,16,32,256]{3,2,1,0:T(8,128)} copy(f32[2,16,32,256]{3,2,1,0:T(8,128)S(1)} %get-tuple-element.15) | data formatting | bytes 2097152
  35.4 0.8 %copy.18 = f32[2,8,32,256]{3,2,1,0:T(8,128)} copy(f32[2,8,32,256]{3,2,1,0:T(8,128)S(1)} %get-tuple-element.16) | data formatting | bytes 1048576
  36.2 0.7 %copy.19 = f32[2,4,32,256]{3,2,1,0:T(8,128)} copy(f32[2,4,32,256]{3,2,1,0:T(8,128)S(1)} %get-tuple-element.17) | data formatting | bytes 524288
  36.9 0.7 %copy.20 = f32[2,2,32,256]{3,2,1,0:T(8,128)} copy(f32[2,2,32,256]{3,2,1,0:T(8,128)S(1)} %get-tuple-element.18) | data formatting | bytes 262144
  37.5 0.7 %copy.21 = f32[2,2,32,256]{3,2,1,0:T(8,128)} copy(f32[2,2,32,256]{3,2,1,0:T(8,128)S(1)} %get-tuple-element.19) | data formatting | bytes 262144
  38.2 0.6 %copy.22 = f32[2,6]{1,0:T(2,128)} copy(f32[2,6]{1,0:T(2,128)S(1)} %get-tuple-element.20) | data formatting | bytes 96
Async XLA Ops:
  0.6 2.2 %copy-start = (f32[2,64,32,256]{3,2,1,0:T(8,128)S(1)}, f32[2,64,32,256]{3,2,1,0:T(8,128)}, u32[]{:S(2)}) copy-start(f32[2,64,32,256]{3,2,1,0:T(8,128)} %fields_ref.1) | copy-start | bytes 12582916
  2.8 0.7 %copy-start.1 = (f32[2]{0:T(128)S(1)}, f32[2]{0:T(128)}, u32[]{:S(2)}) copy-start(f32[2]{0:T(128)} %threshold_ref.1) | copy-start | bytes 28

commit v2 on v1

--- a/solution.py
+++ b/solution.py
@@ -23,7 +23,7 @@
 def kernel(
     gz_count,
     xy_count,
-    threshold_ref,
+    threshold_hbm,
     fields_ref,
     *refs,
 ):
@@ -31,7 +31,9 @@
     energy_ref = refs[LEVELS + 1]
     inputs = refs[LEVELS + 2 : 2 * LEVELS + 2]
     send_buf, recv_buf, acc, e_send_buf, e_recv_buf = refs[2 * LEVELS + 2 : 2 * LEVELS + 7]
-    in_sem, edge_sem, send_sem, recv_sem, e_send_sem, e_recv_sem = refs[2 * LEVELS + 7 :]
+    (threshold_ref, in_sem, edge_sem, send_sem, recv_sem, e_send_sem, e_recv_sem, limit_sem) = refs[
+        2 * LEVELS + 7 :
+    ]
     field_count, layers, width, _ = fields_ref.shape
     per_field = width // ROWS
     chunks = field_count * per_field
@@ -45,15 +47,24 @@
     not_first = gz > 0
     not_last = gz < gz_count - 1
 
-    def peer(step):
-        target = lax.rem(me + step, devices)
-        return (target // xy_count, lax.rem(target, xy_count))
+    def wrapped(value, step, count):
+        moved = value + step
+        return jnp.where(moved >= count, moved - count, moved)
+
+    def for_peers(act):
+        for across in range(1, xy_count):
+            act((gz, wrapped(xy, across, xy_count)))
+
+        @pl.loop(1, gz_count)
+        def _(along):
+            for across in range(xy_count):
+                act((wrapped(gz, along, gz_count), wrapped(xy, across, xy_count)))
 
     barrier = pltpu.get_barrier_semaphore()
 
-    @pl.loop(1, devices)
-    def _(step):
-        pl.semaphore_signal(barrier, inc=1, device_id=peer(step), device_id_type=MESH)
+    for_peers(
+        lambda peer: pl.semaphore_signal(barrier, inc=1, device_id=peer, device_id_type=MESH)
+    )
 
     def place(c):
         return c // per_field, pl.multiple_of(lax.rem(c, per_field) * ROWS, ROWS)
@@ -73,6 +84,8 @@
 
     edge_copy(0).start()
     edge_copy(1).start()
+    limit_copy = pltpu.make_async_copy(threshold_hbm, threshold_ref, limit_sem)
+    limit_copy.start()
 
     @pl.loop(0, chunks)
     def _(c):
@@ -122,7 +135,7 @@
         def _():
             state_copy(level, c, DOWN).wait_recv()
 
-    def full_level(level, c):
+    def lift(level, c, begin, end, low, high, emit_detail, emit_approx):
         source = inputs[level]
         half = source.shape[1] // 2
         final = level == LEVELS - 1
@@ -135,52 +148,68 @@
         for t in range(ROWS // SUB):
             at = pl.ds(pl.multiple_of(row + t * SUB, SUB), SUB)
             to = pl.ds(t * SUB, SUB)
-            low_x = recv_buf[level, UP, c, 0, to]
-            low_y = recv_buf[level, UP, c, 1, to]
-            high_p = recv_buf[level, DOWN, c, 0, to]
-            high_q = recv_buf[level, DOWN, c, 1, to]
-            detail_sum = None
-            coarse_sum = None
-            s = source[f, 0, at]
-            d1_before = s1_before = d2_before = None
-            for i in range(half + 1):
-                if i < half:
+            evens = lambda i: source[f, 2 * i, at]
+            odds = lambda i: source[f, 2 * i + 1, at]
+            d1, s1, d2, sums = {}, {}, {}, {}
+
+            def emit(kind, ref, i, value):
+                band = shrink(value)
+                ref[f, i, at] = band
+                square = band * band
+                sums[kind] = sums[kind] + square if kind in sums else square
+
+            s = evens(begin)
+            for i in range(begin, end + 1):
+                if i < end:
                     if i + 1 < half:
-                        s_next = source[f, 2 * i + 2, at]
+                        s_next = evens(i + 1)
                     else:
-                        s_next = jnp.where(last, s, high_p)
-                    d1 = source[f, 2 * i + 1, at] + ALPHA * (s + s_next)
-                    if i == 0:
-                        d1_before = jnp.where(first, d1, low_x + ALPHA * s)
-                    s1 = s + BETA * (d1_before + d1)
-                else:
-                    s1 = jnp.where(last, s1_before, high_q + BETA * d1_before)
-                if i == 0:
-                    outer = low_y + BETA * d1_before
-                    d2_before = d1_before + GAMMA * (outer + s1)
-                else:
-                    d2 = d1_before + GAMMA * (s1_before + s1)
-                    if i == 1:
-                        d2_before = jnp.where(first, d2, d2_before)
-                    s2 = s1_before + DELTA * (d2_before + d2)
-                    band = shrink(d2 * (KAPPA / SQRT_TWO))
-                    outs[level][f, i - 1, at] = band
-                    square = band * band
-                    detail_sum = square if detail_sum is None else detail_sum + square
-                    approx = s2 * (SQRT_TWO / KAPPA)
-                    if final:
-                        band = shrink(approx)
-                        outs[LEVELS][f, i - 1, at] = band
-                        square = band * band
-                        coarse_sum = square if coarse_sum is None else coarse_sum + square
-                    else:
-                        inputs[level + 1][f, i - 1, at] = approx
-                    d2_before = d2
-                if i < half:
-                    d1_before, s1_before, s = d1, s1, s_next
-            acc[f, level] += detail_sum
-            if final:
-                acc[f, LEVELS] += coarse_sum
+                        s_next = jnp.where(last, s, recv_buf[level, DOWN, c, 0, to])
+                    d1[i] = odds(i) + ALPHA * (s + s_next)
+                    if i == begin and low:
+                        outer = recv_buf[level, UP, c, 0, to] + ALPHA * s
+                        d1[i - 1] = jnp.where(first, d1[i], outer)
+                    if i - 1 in d1:
+                        s1[i] = s + BETA * (d1[i - 1] + d1[i])
+                    if i == begin and low:
+                        s1[i - 1] = recv_buf[level, UP, c, 1, to] + BETA * d1[i - 1]
+                        d2[i - 1] = d1[i - 1] + GAMMA * (s1[i - 1] + s1[i])
+                    s = s_next
+                elif high:
+                    outer = recv_buf[level, DOWN, c, 1, to] + BETA * d1[i - 1]
+                    s1[i] = jnp.where(last, s1[i - 1], outer)
+                if i > begin and i - 1 in s1 and i in s1:
+                    d2[i - 1] = d1[i - 1] + GAMMA * (s1[i - 1] + s1[i])
+                    if i - 1 == begin and low:
+                        d2[i - 2] = jnp.where(first, d2[i - 1], d2[i - 2])
+                    if i - 1 in emit_detail:
+                        emit(level, outs[level], i - 1, d2[i - 1] * (KAPPA / SQRT_TWO))
+                    if i - 1 in emit_approx:
+                        s2 = s1[i - 1] + DELTA * (d2[i - 2] + d2[i - 1])
+                        approx = s2 * (SQRT_TWO / KAPPA)
+                        if final:
+                            emit(LEVELS, outs[LEVELS], i - 1, approx)
+                        else:
+                            inputs[level + 1][f, i - 1, at] = approx
+            for kind, total in sums.items():
+                acc[f, kind] += total
+
+    def halves_of(level):
+        half = inputs[level].shape[1] // 2
+        return half, half >= 8
+
+    def interior(level, c):
+        half, split = halves_of(level)
+        if split:
+            lift(level, c, 0, half - 1, False, False, range(1, half - 2), range(2, half - 2))
+
+    def rim(level, c):
+        half, split = halves_of(level)
+        if split:
+            lift(level, c, 0, 4, True, False, range(0, 1), range(0, 2))
+            lift(level, c, half - 5, half, False, True, range(half - 2, half), range(half - 2, half))
+        else:
+            lift(level, c, 0, half, True, True, range(half), range(half))
 
     edge_copy(0).wait()
     edge_copy(1).wait()
@@ -189,23 +218,28 @@
     def _(c):
         send_states(0, c)
 
+    limit_copy.wait()
     pl.semaphore_wait(barrier, devices - 1)
 
     @pl.loop(0, chunks)
     def _(c):
         start_states(0, c)
+
+    @pl.loop(0, chunks)
+    def _(c):
+        body_copy(c).wait()
+        interior(0, c)
 
     for level in range(LEVELS):
 
         @pl.loop(0, chunks)
         def _(c):
-            if level == 0:
-                body_copy(c).wait()
             wait_states(level, c)
-            full_level(level, c)
+            rim(level, c)
             if level + 1 < LEVELS:
                 send_states(level + 1, c)
                 start_states(level + 1, c)
+                interior(level + 1, c)
 
     lane = lax.broadcasted_iota(jnp.int32, (1, 128), 1)
     for f in range(field_count):
@@ -215,19 +249,17 @@
             row = jnp.where(lane == b, total, row)
         e_send_buf[pl.ds(f, 1), :] = row
 
-    def energy_copy(step):
+    def energy_copy(peer):
         return pltpu.make_async_remote_copy(
             src_ref=e_send_buf,
             dst_ref=e_recv_buf.at[me],
             send_sem=e_send_sem,
             recv_sem=e_recv_sem,
-            device_id=peer(step),
+            device_id=peer,
             device_id_type=MESH,
         )
 
-    @pl.loop(1, devices)
-    def _(step):
-        energy_copy(step).start()
+    for_peers(lambda peer: energy_copy(peer).start())
 
     e_recv_buf[me] = e_send_buf[...]
 
@@ -254,6 +286,19 @@
             @pl.when(not_first)
             def _():
                 state_copy(level, c, DOWN).wait_send()
+
+
+def write_out(*refs):
+    count = (len(refs) - 1) // 2
+    sources, targets, sems = refs[:count], refs[count : 2 * count], refs[-1]
+    copies = [
+        pltpu.make_async_copy(source, target, sems.at[k])
+        for k, (source, target) in enumerate(zip(sources, targets))
+    ]
+    for copy in copies:
+        copy.start()
+    for copy in copies:
+        copy.wait()
 
 
 def solution(mesh):
@@ -267,15 +312,15 @@
         halves = [layers >> (level + 1) for level in range(LEVELS)]
         band_layers = halves + halves[-1:]
         vmem = pl.BlockSpec(memory_space=pltpu.VMEM)
-        return pl.pallas_call(
+        shapes = tuple(
+            jax.ShapeDtypeStruct((field_count, n, width, depth), f32) for n in band_layers
+        ) + (jax.ShapeDtypeStruct((field_count, LEVELS + 1), f32),)
+        results = pl.pallas_call(
             functools.partial(kernel, gz_count, xy_count),
-            out_shape=tuple(
-                jax.ShapeDtypeStruct((field_count, n, width, depth), f32) for n in band_layers
-            )
-            + (jax.ShapeDtypeStruct((field_count, LEVELS + 1), f32),),
+            out_shape=tuple(pltpu.VMEM(shape.shape, shape.dtype) for shape in shapes),
             in_specs=[
-                pl.BlockSpec(memory_space=pltpu.SMEM),
-                pl.BlockSpec(memory_space=pl.ANY),
+                pl.BlockSpec(memory_space=pltpu.HBM),
+                pl.BlockSpec(memory_space=pltpu.HBM),
             ],
             out_specs=(vmem,) * (LEVELS + 2),
             scratch_shapes=[
@@ -287,10 +332,12 @@
                 pltpu.VMEM((field_count, LEVELS + 1, SUB, depth), f32),
                 pltpu.VMEM((field_count, 128), f32),
                 pltpu.VMEM((devices, field_count, 128), f32),
+                pltpu.SMEM((field_count,), f32),
                 pltpu.SemaphoreType.DMA((chunks,)),
                 pltpu.SemaphoreType.DMA((2,)),
                 pltpu.SemaphoreType.DMA((LEVELS, 2, chunks)),
                 pltpu.SemaphoreType.DMA((LEVELS, 2, chunks)),
+                pltpu.SemaphoreType.DMA,
                 pltpu.SemaphoreType.DMA,
                 pltpu.SemaphoreType.DMA,
             ],
@@ -299,7 +346,18 @@
                 has_side_effects=True,
                 vmem_limit_bytes=32 * 1024 * 1024,
             ),
-        )(threshold, fields)
+        )(
+            pltpu.with_memory_space_constraint(threshold, pltpu.HBM),
+            pltpu.with_memory_space_constraint(fields, pltpu.HBM),
+        )
+        return pl.pallas_call(
+            write_out,
+            out_shape=shapes,
+            in_specs=[vmem] * (LEVELS + 2),
+            out_specs=(pl.BlockSpec(memory_space=pltpu.HBM),) * (LEVELS + 2),
+            scratch_shapes=[pltpu.SemaphoreType.DMA((LEVELS + 2,))],
+            compiler_params=pltpu.CompilerParams(vmem_limit_bytes=4 * 1024 * 1024),
+        )(*(pltpu.with_memory_space_constraint(result, pltpu.VMEM) for result in results))
 
     banded = P(None, "gz", "xy", None)
     return jax.shard_map(

time: 38.9 us -> 30.9 us (0.79)
  local copies, waits for them, and re-layouts: 8.49 us -> 0 us
  Pallas kernels: 29.6 us -> 30.1 us
    unnamed x11 -> x0, local copies, waits for them, and re-layouts: 8.49 us -> none
    pallas_call x0 -> x1, Pallas kernels: none -> 2.06 us  [local(): pl.pallas_call(write_out, out_shape=shapes, in_specs=[vmem] * (LEVELS + 2...]
    pallas_call x1, Pallas kernels: 29.6 us -> 28.1 us  [local(): pl.pallas_call(functools.partial(kernel, gz_count, xy_count), out_shape=t...]
where the time goes in v2:
time: 30.9 us; the launch traced here: 30.8 us
  Pallas kernels  30.1 us (97%)
  between operations  0.64 us (2%)
    pallas_call x1, Pallas kernels, local(): pl.pallas_call(functools.partial(kernel, gz_count, xy_count), out_shape=t...  28.1 us
    pallas_call x1, Pallas kernels, local(): pl.pallas_call(write_out, out_shape=shapes, in_specs=[vmem] * (LEVELS + 2...  2.06 us

profile of v2, /device:TPU:0, one launch (start us, length us, event | category | flops | bytes accessed | tf_op | source)
XLA Modules:
  0.0 30.8 jit_solution(13095437468808429185)
XLA Ops:
  0.6 28.1 %shard_map.81 = (f32[2,32,32,256]{3,2,1,0:T(8,128)S(1)}, f32[2,16,32,256]{3,2,1,0:T(8,128)S(1)}, f32[2,8,32,256]{3,2,1,0:T(8,128)S(1)}, f32[2,4,32,256]{3,2,1,0:...) custom-call(f32[2]{0:T(128)} %threshold_hbm.1, ...), custom_call_target="tpu_custom_call" | custom-call | tf_op jit(solution)/shard_map/pallas_call | solution.py:318
  28.7 2.1 %shard_map.82 = (f32[2,32,32,256]{3,2,1,0:T(8,128)}, f32[2,16,32,256]{3,2,1,0:T(8,128)}, f32[2,8,32,256]{3,2,1,0:T(8,128)}, f32[2,4,32,256]{3,2,1,0:T(8,128)}, f...) custom-call(f32[2,32,32,256]{3,2,1,0:T(8,128)S(1)} %get-tuple-element.14.refs_0_, ...), custom_call_target="tpu_custom_call" | custom-call | tf_op jit(solution)/shard_map/pallas_call | solution.py:353

commit v3 on v2

--- a/solution.py
+++ b/solution.py
@@ -17,7 +17,7 @@
 MESH = pl.DeviceIdType.MESH
 UP, DOWN = 0, 1
 SUB = 8
-ROWS = 8
+ROWS = 16
 
 
 def kernel(
@@ -62,9 +62,6 @@
 
     barrier = pltpu.get_barrier_semaphore()
 
-    for_peers(
-        lambda peer: pl.semaphore_signal(barrier, inc=1, device_id=peer, device_id_type=MESH)
-    )
 
     def place(c):
         return c // per_field, pl.multiple_of(lax.rem(c, per_field) * ROWS, ROWS)
@@ -86,6 +83,9 @@
     edge_copy(1).start()
     limit_copy = pltpu.make_async_copy(threshold_hbm, threshold_ref, limit_sem)
     limit_copy.start()
+    for_peers(
+        lambda peer: pl.semaphore_signal(barrier, inc=1, device_id=peer, device_id_type=MESH)
+    )
 
     @pl.loop(0, chunks)
     def _(c):
@@ -230,7 +230,18 @@
         body_copy(c).wait()
         interior(0, c)
 
+    lane = lax.broadcasted_iota(jnp.int32, (1, 128), 1)
+
+    def reduced(f, row, kinds):
+        for b in kinds:
+            total = jnp.sum(jnp.sum(acc[f, b], axis=0, keepdims=True), axis=1, keepdims=True)
+            row = jnp.where(lane == b, total, row)
+        return row
+
+    rows = [jnp.zeros((1, 128), jnp.float32)] * field_count
     for level in range(LEVELS):
+        if level == LEVELS - 1:
+            rows = [reduced(f, row, range(LEVELS - 1)) for f, row in enumerate(rows)]
 
         @pl.loop(0, chunks)
         def _(c):
@@ -241,13 +252,8 @@
                 start_states(level + 1, c)
                 interior(level + 1, c)
 
-    lane = lax.broadcasted_iota(jnp.int32, (1, 128), 1)
-    for f in range(field_count):
-        row = jnp.zeros((1, 128), jnp.float32)
-        for b in range(LEVELS + 1):
-            total = jnp.sum(jnp.sum(acc[f, b], axis=0, keepdims=True), axis=1, keepdims=True)
-            row = jnp.where(lane == b, total, row)
-        e_send_buf[pl.ds(f, 1), :] = row
+    for f, row in enumerate(rows):
+        e_send_buf[pl.ds(f, 1), :] = reduced(f, row, range(LEVELS - 1, LEVELS + 1))
 
     def energy_copy(peer):
         return pltpu.make_async_remote_copy(
@@ -263,6 +269,18 @@
 
     e_recv_buf[me] = e_send_buf[...]
 
+    @pl.loop(0, chunks)
+    def _(c):
+        for level in range(LEVELS):
+
+            @pl.when(not_last)
+            def _():
+                state_copy(level, c, UP).wait_send()
+
+            @pl.when(not_first)
+            def _():
+                state_copy(level, c, DOWN).wait_send()
+
     others = e_recv_buf.at[pl.ds(0, devices - 1)]
     pltpu.make_async_copy(others, others, e_recv_sem).wait()
 
@@ -274,18 +292,6 @@
     energy_ref[...] = (totals / cells)[:, : LEVELS + 1]
 
     pltpu.make_async_copy(others, others, e_send_sem).wait()
-
-    @pl.loop(0, chunks)
-    def _(c):
-        for level in range(LEVELS):
-
-            @pl.when(not_last)
-            def _():
-                state_copy(level, c, UP).wait_send()
-
-            @pl.when(not_first)
-            def _():
-                state_copy(level, c, DOWN).wait_send()
 
 
 def write_out(*refs):

time: 30.9 us -> 30.6 us (level)
    pallas_call x1, Pallas kernels: 28.1 us -> 27.8 us  [local(): pl.pallas_call(functools.partial(kernel, gz_count, xy_count), out_shape=t...]
where the time goes in v3:
time: 30.6 us; the launch traced here: 30.5 us
  Pallas kernels  29.8 us (97%)
  between operations  0.64 us (2%)
    pallas_call x1, Pallas kernels, local(): pl.pallas_call(functools.partial(kernel, gz_count, xy_count), out_shape=t...  27.8 us
    pallas_call x1, Pallas kernels, local(): pl.pallas_call(write_out, out_shape=shapes, in_specs=[vmem] * (LEVELS + 2...  2.06 us

profile of v3, /device:TPU:0, one launch (start us, length us, event | category | flops | bytes accessed | tf_op | source)
XLA Modules:
  0.0 30.5 jit_solution(14386387629205533770)
XLA Ops:
  0.6 27.8 %shard_map.81 = (f32[2,32,32,256]{3,2,1,0:T(8,128)S(1)}, f32[2,16,32,256]{3,2,1,0:T(8,128)S(1)}, f32[2,8,32,256]{3,2,1,0:T(8,128)S(1)}, f32[2,4,32,256]{3,2,1,0:...) custom-call(f32[2]{0:T(128)} %threshold_hbm.1, ...), custom_call_target="tpu_custom_call" | custom-call | tf_op jit(solution)/shard_map/pallas_call | solution.py:324
  28.4 2.1 %shard_map.82 = (f32[2,32,32,256]{3,2,1,0:T(8,128)}, f32[2,16,32,256]{3,2,1,0:T(8,128)}, f32[2,8,32,256]{3,2,1,0:T(8,128)}, f32[2,4,32,256]{3,2,1,0:T(8,128)}, f...) custom-call(f32[2,32,32,256]{3,2,1,0:T(8,128)S(1)} %get-tuple-element.14.refs_0_, ...), custom_call_target="tpu_custom_call" | custom-call | tf_op jit(solution)/shard_map/pallas_call | solution.py:359
